TPU v7x, 32 devices: a whole 2x2x4 slice. The times are simulated.
32 devices in a mesh: grp: 4 (over x, core), mem: 8 (over z, y).
Axes of the slice: x: 2, y: 2, z: 4, core: 2. Of those that a mesh axis runs over, the one named last changes fastest.
Arguments:
- perturb: float32 [32, 1024, 1024], P(('grp', 'mem')), may hold values from -0.1875 to 0.1875
- touched_vertex_index: int32 [32, 4, 64], P(('grp', 'mem')), may hold values from 0 to 1023
- proposed_spin_values: int32 [32, 4, 64], P(('grp', 'mem')), may hold values from 0 to 1
- accept: int32 [32, 4, 64], P(('grp', 'mem')), may hold values 0 or 1
- vertex_site_index: int32 [32, 1024], P(('grp', 'mem')), may hold values from 0 to 63
- vertex_time_index: int32 [32, 1024], P(('grp', 'mem')), may hold values from 0 to 4095
- left_proj: float32 [64, 1024], replicated, may hold values from -0.06 to 0.06
- right_proj: float32 [64, 1024], replicated, may hold values from -0.06 to 0.06
- weights: float32 [32], P(('grp', 'mem')), may hold values from 0.3 to 3
- routing: int32 [32, 1], P(('grp', 'mem')), may hold values from 0 to 7; in each aligned block of 8 rows (0 to 7, 8 to 15, ...) at most 2 rows name the same one
- vertex_function_total: float32 [16, 4096, 4096], P('grp', 'mem'), may hold values from -6 to 6
Outputs:
- four_point_out: float32 [16, 4096, 4096], P('grp', 'mem')
Inputs may be any that keep to these rules, and one draw needn't show every extreme that they name: `routing`: among the 8 walkers of one group no member index is named by more than 2 walkers, and in some group one index is named by exactly 2.
All inputs are finite; a program needn't handle non-finite values. No bound on the sum of `accept` on one device may be relied on, other than what follows from the above.
Results may differ from a plain program's by a relative error of at most 0.0003.
Values sent between devices are 32-bit elements; how exact they have to be, the bound alone decides.
A program may use at most 128 MiB of HBM per device.

v0:
```python
import jax
import jax.numpy as jnp
from jax import lax
from jax.sharding import PartitionSpec as P

K = 1024
SITES = 64
LEG = 64
Q = 16
TIMES = 4096
UPDATES = 4
EXACT_ARITHMETIC = lax.Precision.HIGHEST


def legendre(time_ids):
    abscissa = (2.0 * time_ids.astype(jnp.float32) + 1.0) / TIMES - 1.0
    polys = [jnp.ones_like(abscissa), abscissa]
    for degree in range(1, LEG - 1):
        polys.append(
            ((2 * degree + 1) * abscissa * polys[degree] - degree * polys[degree - 1])
            / (degree + 1)
        )
    norms = jnp.sqrt(2.0 * jnp.arange(LEG, dtype=jnp.float32) + 1.0)
    return jnp.stack(polys[:LEG], axis=1) * norms[None, :]


def make_onehot(site_ids):
    return (site_ids[:, None] == jnp.arange(SITES, dtype=jnp.int32)[None, :]).astype(jnp.float32)


def project(onehot, polys, table):
    spread = jnp.dot(onehot, table, precision=EXACT_ARITHMETIC, preferred_element_type=jnp.float32)
    return jnp.sum(spread.reshape(-1, LEG, Q) * polys[:, :, None], axis=1)


def transform(onehot, polys, values):
    weighted = (polys[:, :, None] * values[:, None, :]).reshape(-1, LEG * Q)
    summed = jnp.dot(
        onehot.T, weighted, precision=EXACT_ARITHMETIC, preferred_element_type=jnp.float32
    )
    return summed.reshape(SITES, LEG, Q).transpose(2, 0, 1).reshape(Q, SITES * LEG)


def update_walker(perturb, touched_vertex_index, proposed_spin_values, accept):
    matrix = jnp.eye(K, dtype=jnp.float32) + perturb
    gammas = accept.astype(jnp.float32) * jnp.where(proposed_spin_values == 1, 0.6, -0.4).astype(
        jnp.float32
    )
    positions = jnp.arange(K, dtype=jnp.int32)

    def apply_update(update, matrix):
        chosen = touched_vertex_index[update]
        unit_cols = (positions[:, None] == chosen[None, :]).astype(jnp.float32)
        columns = (jnp.take(matrix, chosen, axis=1) - unit_cols) * gammas[update][None, :]
        row_block = jnp.take(matrix, chosen, axis=0)
        return matrix - jnp.dot(
            columns, row_block, precision=EXACT_ARITHMETIC, preferred_element_type=jnp.float32
        )

    return lax.fori_loop(0, UPDATES, apply_update, matrix)


def reduce_measured_rows(rescaled_rows, right_observed, vertex_function_total):
    left_q, right_q = (
        lax.all_to_all(rescaled_rows, "grp", split_axis=1, concat_axis=0, tiled=True),
        lax.all_to_all(right_observed, "grp", split_axis=1, concat_axis=0, tiled=True),
    )
    left_rows = lax.all_to_all(left_q, "mem", split_axis=2, concat_axis=0, tiled=True)
    return vertex_function_total + jnp.einsum(
        "mqr,mqc->qrc",
        left_rows,
        lax.all_gather(right_q, "mem", axis=0, tiled=True),
        precision=EXACT_ARITHMETIC,
    )


def per_device(
    perturb,
    touched_vertex_index,
    proposed_spin_values,
    accept,
    vertex_site_index,
    vertex_time_index,
    left_proj,
    right_proj,
    weights,
    routing,
    vertex_function_total,
):
    matrix = update_walker(perturb[0], touched_vertex_index[0], proposed_spin_values[0], accept[0])
    polys = legendre(vertex_time_index[0])
    onehot = make_onehot(vertex_site_index[0])
    left_vec = project(onehot, polys, left_proj)
    right_vec = project(onehot, polys, right_proj)
    left_image = jnp.dot(
        matrix, left_vec, precision=EXACT_ARITHMETIC, preferred_element_type=jnp.float32
    )
    right_image = jnp.dot(
        matrix.T, right_vec, precision=EXACT_ARITHMETIC, preferred_element_type=jnp.float32
    )
    member_mask = (jnp.arange(lax.axis_size("mem"), dtype=jnp.int32) == routing[0, 0]).astype(
        jnp.float32
    )
    totals = lax.psum(member_mask * weights[0], "mem")
    own_total = jnp.sum(totals * member_mask)
    gamma_factor_list = weights / own_total
    left_observed = transform(onehot, polys, left_image)[None]
    right_observed = transform(onehot, polys, right_image)[None]
    rescaled_rows = left_observed * gamma_factor_list[:, None, None]
    return reduce_measured_rows(rescaled_rows, right_observed, vertex_function_total)


def solution(mesh):
    in_specs = (
        P(("grp", "mem"), None, None),
        P(("grp", "mem"), None, None),
        P(("grp", "mem"), None, None),
        P(("grp", "mem"), None, None),
        P(("grp", "mem"), None),
        P(("grp", "mem"), None),
        P(),
        P(),
        P(("grp", "mem")),
        P(("grp", "mem"), None),
        P("grp", "mem", None),
    )
    out_specs = P("grp", "mem", None)
    return jax.shard_map(
        per_device, mesh=mesh, in_specs=in_specs, out_specs=out_specs, check_vma=False
    )
```

profile of v0, /device:TPU:0, one launch (start us, length us, event | category | flops | bytes accessed | tf_op | source)
XLA Modules:
  0.0 259.0 jit_solution(9554184018250131046)
XLA Ops:
  7.9 4.9 %bitcast_add_fusion = f32[1024,1024]{1,0:T(8,128)} fusion(f32[1,1024,1024]{2,1,0:T(8,128)} %param.13), kind=kLoop, calls=%fused_computation.24 | loop fusion | flops 3145728 | bytes 8388608 | tf_op jit(solution)/shard_map/add | solution.py:45
  12.8 73.3 %while.14 = (s32[]{:T(128)}, f32[1024,1024]{1,0:T(8,128)}, s32[4,64]{1,0:T(4,128)S(1)}, f32[4,64]{1,0:T(4,128)S(1)}, s32[]{:T(128)}) while((s32[]{:T(128)}, f32[1024,1024]{1,0:T(8,128)}, s32[4,64]{1,0:T(4,128)S(1)}, f32[4,64]{1,0:T(4,128)S(1)}, s32[]{:T(128)}) %tuple.131), condition=%wide.region_1.2_spmd.clone, body=%wide.region_0.1_spmd.clone.sunk | while | flops 806749760 | bytes 18357200 | solution.py:60
  12.9 3.0 %gather_fusion.1 = f32[64,1024]{1,0:T(8,128)S(1)} fusion(f32[1024,1024]{1,0:T(8,128)} %get-tuple-element.275, s32[1024]{0:T(1024)S(1)} %pad_clamp_fusion.2), kind=kCustom, calls=%fused_computation.1.clone.clone.1 | custom fusion | bytes 524544 | tf_op jit(solution)/shard_map/while/body/eval_jaxpr/jit(_take)/gather | solution.py:55
  15.9 5.4 %copy.43 = f32[1024,1024]{0,1:T(8,128)} copy(f32[1024,1024]{1,0:T(8,128)} %get-tuple-element.275) | data formatting | bytes 8388608 | tf_op jit(solution)/shard_map/while
  21.3 3.0 %gather_fusion = f32[64,1024]{1,0:T(8,128)S(1)} fusion(f32[1024,1024]{0,1:T(8,128)} %copy.43, s32[1024]{0:T(1024)S(1)} %pad_clamp_fusion.2), kind=kCustom, calls=%fused_computation.clone.clone.1 | custom fusion | bytes 524544 | tf_op jit(solution)/shard_map/while/body/eval_jaxpr/jit(_take)/gather | solution.py:54
  24.2 6.8 %convolution_subtract_fusion.2 = f32[1024,1024]{1,0:T(8,128)} fusion(f32[1024,1024]{1,0:T(8,128)} %get-tuple-element.275, f32[64,1024]{1,0:T(8,128)S(1)} %gather_fusion, f32[64,1024]{1,0:T(8,128)S(1)} %gather_fusion.1, f32[64]{0:T(128)S(1)} %dynamic-slice_bitcast_fusion.2, s32[64]{0:T(128)S(1)} %get-tuple-element.267, ...), kind=kOutput, calls=%fused_computation.3.clone.1 | convolution fusion | flops 806748160 | bytes 8913472 | tf_op jit(solution)/shard_map/while/body/eval_jaxpr/dot_general | solution.py:56
  31.1 3.0 %gather_fusion.1 = f32[64,1024]{1,0:T(8,128)S(1)} fusion(f32[1024,1024]{1,0:T(8,128)} %get-tuple-element.275, s32[1024]{0:T(1024)S(1)} %pad_clamp_fusion.2), kind=kCustom, calls=%fused_computation.1.clone.clone.1 | custom fusion | bytes 524544 | tf_op jit(solution)/shard_map/while/body/eval_jaxpr/jit(_take)/gather | solution.py:55
  34.1 5.4 %copy.43 = f32[1024,1024]{0,1:T(8,128)} copy(f32[1024,1024]{1,0:T(8,128)} %get-tuple-element.275) | data formatting | bytes 8388608 | tf_op jit(solution)/shard_map/while
  39.5 3.0 %gather_fusion = f32[64,1024]{1,0:T(8,128)S(1)} fusion(f32[1024,1024]{0,1:T(8,128)} %copy.43, s32[1024]{0:T(1024)S(1)} %pad_clamp_fusion.2), kind=kCustom, calls=%fused_computation.clone.clone.1 | custom fusion | bytes 524544 | tf_op jit(solution)/shard_map/while/body/eval_jaxpr/jit(_take)/gather | solution.py:54
  42.4 6.8 %convolution_subtract_fusion.2 = f32[1024,1024]{1,0:T(8,128)} fusion(f32[1024,1024]{1,0:T(8,128)} %get-tuple-element.275, f32[64,1024]{1,0:T(8,128)S(1)} %gather_fusion, f32[64,1024]{1,0:T(8,128)S(1)} %gather_fusion.1, f32[64]{0:T(128)S(1)} %dynamic-slice_bitcast_fusion.2, s32[64]{0:T(128)S(1)} %get-tuple-element.267, ...), kind=kOutput, calls=%fused_computation.3.clone.1 | convolution fusion | flops 806748160 | bytes 8913472 | tf_op jit(solution)/shard_map/while/body/eval_jaxpr/dot_general | solution.py:56
  49.3 3.0 %gather_fusion.1 = f32[64,1024]{1,0:T(8,128)S(1)} fusion(f32[1024,1024]{1,0:T(8,128)} %get-tuple-element.275, s32[1024]{0:T(1024)S(1)} %pad_clamp_fusion.2), kind=kCustom, calls=%fused_computation.1.clone.clone.1 | custom fusion | bytes 524544 | tf_op jit(solution)/shard_map/while/body/eval_jaxpr/jit(_take)/gather | solution.py:55
  52.3 5.4 %copy.43 = f32[1024,1024]{0,1:T(8,128)} copy(f32[1024,1024]{1,0:T(8,128)} %get-tuple-element.275) | data formatting | bytes 8388608 | tf_op jit(solution)/shard_map/while
  57.7 3.0 %gather_fusion = f32[64,1024]{1,0:T(8,128)S(1)} fusion(f32[1024,1024]{0,1:T(8,128)} %copy.43, s32[1024]{0:T(1024)S(1)} %pad_clamp_fusion.2), kind=kCustom, calls=%fused_computation.clone.clone.1 | custom fusion | bytes 524544 | tf_op jit(solution)/shard_map/while/body/eval_jaxpr/jit(_take)/gather | solution.py:54
  60.6 6.8 %convolution_subtract_fusion.2 = f32[1024,1024]{1,0:T(8,128)} fusion(f32[1024,1024]{1,0:T(8,128)} %get-tuple-element.275, f32[64,1024]{1,0:T(8,128)S(1)} %gather_fusion, f32[64,1024]{1,0:T(8,128)S(1)} %gather_fusion.1, f32[64]{0:T(128)S(1)} %dynamic-slice_bitcast_fusion.2, s32[64]{0:T(128)S(1)} %get-tuple-element.267, ...), kind=kOutput, calls=%fused_computation.3.clone.1 | convolution fusion | flops 806748160 | bytes 8913472 | tf_op jit(solution)/shard_map/while/body/eval_jaxpr/dot_general | solution.py:56
  67.5 3.0 %gather_fusion.1 = f32[64,1024]{1,0:T(8,128)S(1)} fusion(f32[1024,1024]{1,0:T(8,128)} %get-tuple-element.275, s32[1024]{0:T(1024)S(1)} %pad_clamp_fusion.2), kind=kCustom, calls=%fused_computation.1.clone.clone.1 | custom fusion | bytes 524544 | tf_op jit(solution)/shard_map/while/body/eval_jaxpr/jit(_take)/gather | solution.py:55
  70.5 5.4 %copy.43 = f32[1024,1024]{0,1:T(8,128)} copy(f32[1024,1024]{1,0:T(8,128)} %get-tuple-element.275) | data formatting | bytes 8388608 | tf_op jit(solution)/shard_map/while
  78.9 6.8 %convolution_subtract_fusion.2 = f32[1024,1024]{1,0:T(8,128)} fusion(f32[1024,1024]{1,0:T(8,128)} %get-tuple-element.275, f32[64,1024]{1,0:T(8,128)S(1)} %gather_fusion, f32[64,1024]{1,0:T(8,128)S(1)} %gather_fusion.1, f32[64]{0:T(128)S(1)} %dynamic-slice_bitcast_fusion.2, s32[64]{0:T(128)S(1)} %get-tuple-element.267, ...), kind=kOutput, calls=%fused_computation.3.clone.1 | convolution fusion | flops 806748160 | bytes 8913472 | tf_op jit(solution)/shard_map/while/body/eval_jaxpr/dot_general | solution.py:56
  86.2 3.8 %fusion.28 = f32[1024,1024]{0,1:T(8,128)} fusion(f32[64,1024]{1,0:T(8,128)S(1)} %copy-done, s32[1024]{0:T(1024)S(1)} %bitcast.184), kind=kOutput, calls=%fused_computation.39 | convolution fusion | flops 805371904 | bytes 4460544 | tf_op jit(solution)/shard_map/dot_general | solution.py:32
  90.0 3.8 %fusion.30 = f32[1024,1024]{0,1:T(8,128)} fusion(f32[64,1024]{1,0:T(8,128)S(1)} %copy-done.3, s32[1024]{0:T(1024)S(1)} %bitcast.185), kind=kOutput, calls=%fused_computation.41 | convolution fusion | flops 805371904 | bytes 4460544 | tf_op jit(solution)/shard_map/dot_general | solution.py:32
  94.8 4.7 %multiply_reduce_fusion = (f32[1024,16]{0,1:T(8,128)S(1)}, f32[1024,16]{0,1:T(8,128)S(1)}) fusion(f32[1024,64,16]{0,2,1:T(8,128)} %bitcast.178, f32[1024,64]{0,1:T(8,128)S(1)} %broadcast_multiply_fusion, f32[1024,64,16]{0,2,1:T(8,128)} %bitcast.179), kind=kLoop, calls=%fused_computation.30 | loop fusion | flops 4161536 | bytes 8781824 | tf_op jit(solution)/shard_map/reduce_sum | solution.py:33
  101.8 3.6 %fusion.41 = f32[1024,16]{0,1:T(8,128)S(1)} fusion(f32[1024,1024]{1,0:T(8,128)S(1)} %copy-done.2, f32[1024,16]{0,1:T(8,128)S(1)} %get-tuple-element.111), kind=kOutput, calls=%fused_computation.217 | convolution fusion | flops 201326592 | bytes 4325376 | tf_op jit(solution)/shard_map/dot_general | solution.py:95
  108.1 5.6 %fusion.19 = f32[16,64,64]{2,1,0:T(8,128)S(1)} fusion(f32[64,16,1024]{2,1,0:T(8,128)S(1)} %get-tuple-element.173, s32[1024]{0:T(1024)S(1)} %bitcast.186), kind=kOutput, calls=%fused_computation.35 | convolution fusion | flops 805371904 | bytes 4460544 | tf_op jit(solution)/shard_map/dot_general | solution.py:38
  114.0 10.0 %all_to_all.42 = f32[1,16,4096]{2,0,1:T(1,128)S(1)} all-to-all(f32[1,16,4096]{2,0,1:T(1,128)S(1)} %broadcast_in_dim_reshape.5), channel_id=1, replica_groups=mesh['grp'=4,'mem'=8] {'grp'}, dimensions={1} | all-to-all | bytes 524288 | tf_op jit(solution)/shard_map/all_to_all | solution.py:66
  126.8 21.8 %psum.7 = f32[8]{0:T(128)S(1)} all-reduce(f32[8]{0:T(128)S(1)} %compare_select_fusion.3), channel_id=1, replica_groups=mesh['grp'=4,'mem'=8] {'mem'}, use_global_device_ids=true, to_apply=%region_3.4 | all-reduce | flops 8 | bytes 64 | tf_op jit(solution)/shard_map/psum | solution.py:104
  150.0 7.4 %fusion.25 = f32[16,64,64]{2,1,0:T(8,128)S(1)} fusion(f32[64,16,1024]{2,1,0:T(8,128)} %get-tuple-element.174, f32[]{:T(128)} %bitcast.34, s32[1024]{0:T(1024)S(1)} %bitcast.187), kind=kOutput, calls=%fused_computation.37 | convolution fusion | flops 805437440 | bytes 4460548 | tf_op jit(solution)/shard_map/dot_general | solution.py:38
  157.7 8.6 %all_to_all.43 = f32[1,16,4096]{2,0,1:T(1,128)S(1)} all-to-all(f32[1,16,4096]{2,0,1:T(1,128)S(1)} %mul.18371), channel_id=1, replica_groups=mesh['grp'=4,'mem'=8] {'grp'}, dimensions={1} | all-to-all | bytes 524288 | tf_op jit(solution)/shard_map/all_to_all | solution.py:65
  167.0 5.8 %copy.21 = f32[4,4,4096]{1,0,2:T(4,128)} copy(f32[4,4,4096]{2,1,0:T(4,128)S(1)} %all_to_all.32) | data formatting | bytes 524288 | tf_op jit(solution)/shard_map/all_to_all | solution.py:65
  172.8 11.3 %reshape.1435 = f32[8,1,8192]{2,1,0:T(1,128)S(1)} reshape(f32[4096,4,4]{2,1,0:T(4,128)} %bitcast.176) | data formatting | bytes 524288
  184.1 11.6 %all_to_all.44 = f32[8,1,8192]{2,1,0:T(1,128)S(1)} all-to-all(f32[8,1,8192]{2,1,0:T(1,128)S(1)} %reshape.1435), channel_id=1, replica_groups=mesh['grp'=4,'mem'=8] {'mem'}, dimensions={0} | all-to-all | bytes 524288 | tf_op jit(solution)/shard_map/all_to_all | solution.py:68
  197.6 14.2 %reshape.1436 = f32[4096,4,4]{2,1,0:T(4,128)} reshape(f32[8,8192]{1,0:T(8,128)S(1)} %reduce.2) | data formatting | bytes 524288
  211.8 5.2 %copy.27 = f32[4,4,8,512]{3,2,1,0:T(8,128)S(1)} copy(f32[4,4,8,512]{1,0,3,2:T(4,128)} %bitcast.177) | data formatting | bytes 524288 | tf_op jit(solution)/shard_map/all_to_all | solution.py:68
  217.3 34.6 %convolution_add_fusion = f32[4,512,4096]{2,1,0:T(8,128)} fusion(f32[4,512,4096]{2,1,0:T(8,128)} %param.23, f32[32,4,512]{2,0,1:T(8,128)S(1)} %all_to_all.36, f32[32,4,4096]{2,1,0:T(4,128)} %all-gather.2.cloned.1.call-done), kind=kOutput, calls=%fused_computation.23 | convolution fusion | flops 3229614080 | bytes 69468160 | tf_op jit(solution)/shard_map/mqr,mqc->qrc/dot_general | solution.py:69
  (78 shorter events, 15.7 us)
Async XLA Ops:
  6.5 79.6 %copy-start = (f32[64,1024]{1,0:T(8,128)S(1)}, f32[64,1024]{1,0:T(8,128)}, u32[]{:S(2)}) copy-start(f32[64,1024]{1,0:T(8,128)} %param.20) | copy-start | bytes 786436
  6.5 210.8 %all-gather.2.cloned.1.call-start = ((), (), s32[]{:S(2)}) async-start(), calls=%async_computation.3 | async-start | bytes 2359296 | tf_op jit(solution)/shard_map/all_gather | solution.py:72
  7.8 4.9 %copy-start.6 = (s32[1,4,64]{2,1,0:T(4,128)S(1)}, s32[1,4,64]{2,1,0:T(4,128)}, u32[]{:S(2)}) copy-start(s32[1,4,64]{2,1,0:T(4,128)} %param.16) | copy-start | bytes 3076
  7.8 4.9 %copy-start.7 = (s32[1,4,64]{2,1,0:T(4,128)S(1)}, s32[1,4,64]{2,1,0:T(4,128)}, u32[]{:S(2)}) copy-start(s32[1,4,64]{2,1,0:T(4,128)} %param.15) | copy-start | bytes 3076
  7.9 4.9 %copy-start.5 = (s32[1,4,64]{2,1,0:T(4,128)S(1)}, s32[1,4,64]{2,1,0:T(4,128)}, u32[]{:S(2)}) copy-start(s32[1,4,64]{2,1,0:T(4,128)} %param.14) | copy-start | bytes 3076
  12.8 73.4 %copy-start.4 = (s32[1,1024]{1,0:T(1,128)S(1)}, s32[1,1024]{1,0:T(1,128)}, u32[]{:S(2)}) copy-start(s32[1,1024]{1,0:T(1,128)} %param.17) | copy-start | bytes 12292
  86.1 3.8 %copy-start.3 = (f32[64,1024]{1,0:T(8,128)S(1)}, f32[64,1024]{1,0:T(8,128)}, u32[]{:S(2)}) copy-start(f32[64,1024]{1,0:T(8,128)} %param.19) | copy-start | bytes 786436
  94.8 4.7 %copy-start.2 = (f32[1024,1024]{1,0:T(8,128)S(1)}, f32[1024,1024]{1,0:T(8,128)}, u32[]{:S(2)}) copy-start(f32[1024,1024]{1,0:T(8,128)} %get-tuple-element.99) | copy-start | bytes 12582916
  217.3 34.6 %copy-start.1 = (f32[64,1024]{1,0:T(8,128)S(1)}, f32[64,1024]{1,0:T(8,128)}, u32[]{:S(2)}) copy-start(f32[64,1024]{1,0:T(8,128)} %param.20) | copy-start | bytes 786436
Sparse Core Ops, SparseCore 0:
  125.6 49.6 all-gather.1
where the time goes:
time: 263 us; the launch traced here: 259 us
  matrix products  88.3 us (34%)
  local copies, waits for them, and re-layouts  84.9 us (32%)
  blocking collectives  52.1 us (20%)
  other arithmetic  17.1 us (7%)
  between operations  16 us (6%)
    dot_general x1, matrix products, reduce_measured_rows(): jnp.einsum('mqr,mqc->qrc', left_rows, lax.all_gather(right_q, 'mem', axis...  34.6 us
    dot_general x4, matrix products, apply_update(): jnp.dot(columns, row_block, precision=EXACT_ARITHMETIC, preferred_element...  27.2 us
    unnamed x18, local copies, waits for them, and re-layouts  25.6 us
    psum x1, blocking collectives, per_device(): totals = lax.psum(member_mask * weights[0], 'mem')  21.8 us
    while x4, local copies, waits for them, and re-layouts  21.6 us
    dot_general x2, matrix products, transform(): jnp.dot(onehot.T, weighted, precision=EXACT_ARITHMETIC, preferred_element...  13 us
    gather x4, local copies, waits for them, and re-layouts, apply_update(): row_block = jnp.take(matrix, chosen, axis=0)  11.9 us
    gather x4, local copies, waits for them, and re-layouts, apply_update(): jnp.take(matrix, chosen, axis=1) - unit_cols  11.9 us
  transfers between devices with their start and end apart: 1, of which 0 were waited for; matrix products, arithmetic and copies ran while one was open for 18% of the time, Pallas kernels for 0%

commit v1 on v0

--- a/solution.py
+++ b/solution.py
@@ -65,7 +65,16 @@
         lax.all_to_all(rescaled_rows, "grp", split_axis=1, concat_axis=0, tiled=True),
         lax.all_to_all(right_observed, "grp", split_axis=1, concat_axis=0, tiled=True),
     )
-    left_rows = lax.all_to_all(left_q, "mem", split_axis=2, concat_axis=0, tiled=True)
+    _close_target = lambda v0, dim_no, axis_no: jnp.concatenate(
+        lax.all_to_all(
+            jnp.stack(jnp.split(v0, lax.axis_size("mem"), axis=axis_no)),
+            concat_axis=0,
+            axis_name="mem",
+            split_axis=0,
+        ),
+        axis=dim_no,
+    )
+    left_rows = _close_target(left_q, 0, 2)
     return vertex_function_total + jnp.einsum(
         "mqr,mqc->qrc",
         left_rows,

time: 263 us -> 222 us (0.84); the launches traced: 259 us -> 221 us
  local copies, waits for them, and re-layouts: 84.9 us -> 47.6 us
    unnamed x18 -> x23, local copies, waits for them, and re-layouts: 25.6 us -> 0.2 us
    all_to_all x4 -> x1, local copies, waits for them, and re-layouts: 6.01 us -> 0.02 us  [reduce_measured_rows(): lax.all_to_all(jnp.stack(jnp.split(v0, lax.axis_size('mem'), axis=axis_no...]
    all_to_all x2 -> x1, local copies, waits for them, and re-layouts: 5.92 us -> 0.08 us  [reduce_measured_rows(): lax.all_to_all(rescaled_rows, 'grp', split_axis=1, concat_axis=0, tiled=T...]
  transfers between devices with their start and end apart: 1 -> 1, of which waited for: 0 -> 0; matrix products, arithmetic and copies ran while one was open for 18% -> 4% of each run, Pallas kernels for 0% -> 0%
where the time goes in v1:
time: 222 us; the launch traced here: 221 us
  matrix products  88.1 us (40%)
  blocking collectives  53.8 us (24%)
  local copies, waits for them, and re-layouts  47.6 us (21%)
  other arithmetic  15.9 us (7%)
  between operations  15.8 us (7%)
    dot_general x1, matrix products, reduce_measured_rows(): jnp.einsum('mqr,mqc->qrc', left_rows, lax.all_gather(right_q, 'mem', axis...  34.4 us
    dot_general x4, matrix products, apply_update(): jnp.dot(columns, row_block, precision=EXACT_ARITHMETIC, preferred_element...  27.1 us
    psum x1, blocking collectives, per_device(): totals = lax.psum(member_mask * weights[0], 'mem')  21.8 us
    while x4, local copies, waits for them, and re-layouts  21.4 us
    all_to_all x1, blocking collectives, reduce_measured_rows(): lax.all_to_all(jnp.stack(jnp.split(v0, lax.axis_size('mem'), axis=axis_no...  13.6 us
    dot_general x2, matrix products, transform(): jnp.dot(onehot.T, weighted, precision=EXACT_ARITHMETIC, preferred_element...  13 us
    gather x4, local copies, waits for them, and re-layouts, apply_update(): row_block = jnp.take(matrix, chosen, axis=0)  11.9 us
    gather x4, local copies, waits for them, and re-layouts, apply_update(): jnp.take(matrix, chosen, axis=1) - unit_cols  11.9 us
  transfers between devices with their start and end apart: 1, of which 0 were waited for; matrix products, arithmetic and copies ran while one was open for 4% of the time, Pallas kernels for 0%

profile of v1, /device:TPU:0, one launch (start us, length us, event | category | flops | bytes accessed | tf_op | source)
XLA Modules:
  0.0 221.4 jit_solution(5353907965545448806)
XLA Ops:
  6.6 1.1 subtract_multiply_fusion.2
  7.9 4.9 %bitcast_add_fusion = f32[1024,1024]{1,0:T(8,128)} fusion(f32[1,1024,1024]{2,1,0:T(8,128)} %param.13), kind=kLoop, calls=%fused_computation.24 | loop fusion | flops 3145728 | bytes 8388608 | tf_op jit(solution)/shard_map/add | solution.py:45
  12.8 72.7 %while.14 = (s32[]{:T(128)}, f32[1024,1024]{1,0:T(8,128)}, s32[4,64]{1,0:T(4,128)S(1)}, f32[4,64]{1,0:T(4,128)S(1)}, s32[]{:T(128)}) while((s32[]{:T(128)}, f32[1024,1024]{1,0:T(8,128)}, s32[4,64]{1,0:T(4,128)S(1)}, f32[4,64]{1,0:T(4,128)S(1)}, s32[]{:T(128)}) %tuple.138), condition=%wide.region_1.2_spmd.clone, body=%wide.region_0.1_spmd.clone.sunk | while | flops 806749760 | bytes 18357200 | solution.py:60
  12.9 3.0 %gather_fusion.1 = f32[64,1024]{1,0:T(8,128)S(1)} fusion(f32[1024,1024]{1,0:T(8,128)} %get-tuple-element.283, s32[1024]{0:T(1024)S(1)} %pad_clamp_fusion.2), kind=kCustom, calls=%fused_computation.1.clone.clone.1 | custom fusion | bytes 524544 | tf_op jit(solution)/shard_map/while/body/eval_jaxpr/jit(_take)/gather | solution.py:55
  15.9 5.4 %copy.95 = f32[1024,1024]{0,1:T(8,128)} copy(f32[1024,1024]{1,0:T(8,128)} %get-tuple-element.283) | data formatting | bytes 8388608 | tf_op jit(solution)/shard_map/while
  21.2 3.0 %gather_fusion = f32[64,1024]{1,0:T(8,128)S(1)} fusion(f32[1024,1024]{0,1:T(8,128)} %copy.95, s32[1024]{0:T(1024)S(1)} %pad_clamp_fusion.2), kind=kCustom, calls=%fused_computation.clone.clone.1 | custom fusion | bytes 524544 | tf_op jit(solution)/shard_map/while/body/eval_jaxpr/jit(_take)/gather | solution.py:54
  24.2 6.8 %convolution_subtract_fusion.2 = f32[1024,1024]{1,0:T(8,128)} fusion(f32[1024,1024]{1,0:T(8,128)} %get-tuple-element.283, f32[64,1024]{1,0:T(8,128)S(1)} %gather_fusion, f32[64,1024]{1,0:T(8,128)S(1)} %gather_fusion.1, f32[64]{0:T(128)S(1)} %dynamic-slice_bitcast_fusion.2, s32[64]{0:T(128)S(1)} %get-tuple-element.275, ...), kind=kOutput, calls=%fused_computation.3.clone.1 | convolution fusion | flops 806748160 | bytes 8913472 | tf_op jit(solution)/shard_map/while/body/eval_jaxpr/dot_general | solution.py:56
  31.0 3.0 %gather_fusion.1 = f32[64,1024]{1,0:T(8,128)S(1)} fusion(f32[1024,1024]{1,0:T(8,128)} %get-tuple-element.283, s32[1024]{0:T(1024)S(1)} %pad_clamp_fusion.2), kind=kCustom, calls=%fused_computation.1.clone.clone.1 | custom fusion | bytes 524544 | tf_op jit(solution)/shard_map/while/body/eval_jaxpr/jit(_take)/gather | solution.py:55
  34.0 5.4 %copy.95 = f32[1024,1024]{0,1:T(8,128)} copy(f32[1024,1024]{1,0:T(8,128)} %get-tuple-element.283) | data formatting | bytes 8388608 | tf_op jit(solution)/shard_map/while
  39.4 3.0 %gather_fusion = f32[64,1024]{1,0:T(8,128)S(1)} fusion(f32[1024,1024]{0,1:T(8,128)} %copy.95, s32[1024]{0:T(1024)S(1)} %pad_clamp_fusion.2), kind=kCustom, calls=%fused_computation.clone.clone.1 | custom fusion | bytes 524544 | tf_op jit(solution)/shard_map/while/body/eval_jaxpr/jit(_take)/gather | solution.py:54
  42.4 6.8 %convolution_subtract_fusion.2 = f32[1024,1024]{1,0:T(8,128)} fusion(f32[1024,1024]{1,0:T(8,128)} %get-tuple-element.283, f32[64,1024]{1,0:T(8,128)S(1)} %gather_fusion, f32[64,1024]{1,0:T(8,128)S(1)} %gather_fusion.1, f32[64]{0:T(128)S(1)} %dynamic-slice_bitcast_fusion.2, s32[64]{0:T(128)S(1)} %get-tuple-element.275, ...), kind=kOutput, calls=%fused_computation.3.clone.1 | convolution fusion | flops 806748160 | bytes 8913472 | tf_op jit(solution)/shard_map/while/body/eval_jaxpr/dot_general | solution.py:56
  49.2 3.0 %gather_fusion.1 = f32[64,1024]{1,0:T(8,128)S(1)} fusion(f32[1024,1024]{1,0:T(8,128)} %get-tuple-element.283, s32[1024]{0:T(1024)S(1)} %pad_clamp_fusion.2), kind=kCustom, calls=%fused_computation.1.clone.clone.1 | custom fusion | bytes 524544 | tf_op jit(solution)/shard_map/while/body/eval_jaxpr/jit(_take)/gather | solution.py:55
  52.2 5.4 %copy.95 = f32[1024,1024]{0,1:T(8,128)} copy(f32[1024,1024]{1,0:T(8,128)} %get-tuple-element.283) | data formatting | bytes 8388608 | tf_op jit(solution)/shard_map/while
  57.6 3.0 %gather_fusion = f32[64,1024]{1,0:T(8,128)S(1)} fusion(f32[1024,1024]{0,1:T(8,128)} %copy.95, s32[1024]{0:T(1024)S(1)} %pad_clamp_fusion.2), kind=kCustom, calls=%fused_computation.clone.clone.1 | custom fusion | bytes 524544 | tf_op jit(solution)/shard_map/while/body/eval_jaxpr/jit(_take)/gather | solution.py:54
  60.5 6.8 %convolution_subtract_fusion.2 = f32[1024,1024]{1,0:T(8,128)} fusion(f32[1024,1024]{1,0:T(8,128)} %get-tuple-element.283, f32[64,1024]{1,0:T(8,128)S(1)} %gather_fusion, f32[64,1024]{1,0:T(8,128)S(1)} %gather_fusion.1, f32[64]{0:T(128)S(1)} %dynamic-slice_bitcast_fusion.2, s32[64]{0:T(128)S(1)} %get-tuple-element.275, ...), kind=kOutput, calls=%fused_computation.3.clone.1 | convolution fusion | flops 806748160 | bytes 8913472 | tf_op jit(solution)/shard_map/while/body/eval_jaxpr/dot_general | solution.py:56
  67.4 3.0 %gather_fusion.1 = f32[64,1024]{1,0:T(8,128)S(1)} fusion(f32[1024,1024]{1,0:T(8,128)} %get-tuple-element.283, s32[1024]{0:T(1024)S(1)} %pad_clamp_fusion.2), kind=kCustom, calls=%fused_computation.1.clone.clone.1 | custom fusion | bytes 524544 | tf_op jit(solution)/shard_map/while/body/eval_jaxpr/jit(_take)/gather | solution.py:55
  70.4 5.4 %copy.95 = f32[1024,1024]{0,1:T(8,128)} copy(f32[1024,1024]{1,0:T(8,128)} %get-tuple-element.283) | data formatting | bytes 8388608 | tf_op jit(solution)/shard_map/while
  75.7 3.0 %gather_fusion = f32[64,1024]{1,0:T(8,128)S(1)} fusion(f32[1024,1024]{0,1:T(8,128)} %copy.95, s32[1024]{0:T(1024)S(1)} %pad_clamp_fusion.2), kind=kCustom, calls=%fused_computation.clone.clone.1 | custom fusion | bytes 524544 | tf_op jit(solution)/shard_map/while/body/eval_jaxpr/jit(_take)/gather | solution.py:54
  78.7 6.8 %convolution_subtract_fusion.2 = f32[1024,1024]{1,0:T(8,128)} fusion(f32[1024,1024]{1,0:T(8,128)} %get-tuple-element.283, f32[64,1024]{1,0:T(8,128)S(1)} %gather_fusion, f32[64,1024]{1,0:T(8,128)S(1)} %gather_fusion.1, f32[64]{0:T(128)S(1)} %dynamic-slice_bitcast_fusion.2, s32[64]{0:T(128)S(1)} %get-tuple-element.275, ...), kind=kOutput, calls=%fused_computation.3.clone.1 | convolution fusion | flops 806748160 | bytes 8913472 | tf_op jit(solution)/shard_map/while/body/eval_jaxpr/dot_general | solution.py:56
  85.5 3.8 %fusion.28 = f32[1024,1024]{0,1:T(8,128)} fusion(f32[64,1024]{1,0:T(8,128)S(1)} %copy-done, s32[1024]{0:T(1024)S(1)} %bitcast.209), kind=kOutput, calls=%fused_computation.39 | convolution fusion | flops 805371904 | bytes 4460544 | tf_op jit(solution)/shard_map/dot_general | solution.py:32
  89.3 3.8 %fusion.30 = f32[1024,1024]{0,1:T(8,128)} fusion(f32[64,1024]{1,0:T(8,128)S(1)} %copy-done.3, s32[1024]{0:T(1024)S(1)} %bitcast.210), kind=kOutput, calls=%fused_computation.41 | convolution fusion | flops 805371904 | bytes 4460544 | tf_op jit(solution)/shard_map/dot_general | solution.py:32
  94.2 4.7 %multiply_reduce_fusion = (f32[1024,16]{0,1:T(8,128)S(1)}, f32[1024,16]{0,1:T(8,128)S(1)}) fusion(f32[1024,64,16]{0,2,1:T(8,128)} %bitcast.204, f32[1024,64]{0,1:T(8,128)S(1)} %broadcast_multiply_fusion, f32[1024,64,16]{0,2,1:T(8,128)} %bitcast.205), kind=kLoop, calls=%fused_computation.30 | loop fusion | flops 4161536 | bytes 8781824 | tf_op jit(solution)/shard_map/reduce_sum | solution.py:33
  98.9 2.3 %fusion.51 = f32[1024,16]{0,1:T(8,128)S(1)} fusion(f32[1024,1024]{1,0:T(8,128)S(1)} %copy-done.2, f32[1024,16]{0,1:T(8,128)S(1)} %get-tuple-element.110), kind=kOutput, calls=%fused_computation.235 | convolution fusion | flops 201326592 | bytes 4325376 | tf_op jit(solution)/shard_map/dot_general | solution.py:107
  101.2 3.6 %fusion.50 = f32[1024,16]{0,1:T(8,128)S(1)} fusion(f32[1024,1024]{1,0:T(8,128)S(1)} %copy-done.2, f32[1024,16]{0,1:T(8,128)S(1)} %get-tuple-element.111), kind=kOutput, calls=%fused_computation.234 | convolution fusion | flops 201326592 | bytes 4325376 | tf_op jit(solution)/shard_map/dot_general | solution.py:104
  104.8 2.6 %multiply_bitcast_fusion = (f32[64,16,1024]{2,1,0:T(8,128)S(1)}, f32[64,16,1024]{2,1,0:T(8,128)}) fusion(f32[1024,16]{0,1:T(8,128)S(1)} %fusion.51, f32[1024,64]{0,1:T(8,128)S(1)} %broadcast_multiply_fusion, f32[1024,16]{0,1:T(8,128)S(1)} %fusion.50), kind=kLoop, calls=%fused_computation.29 | loop fusion | flops 2097152 | bytes 8781824 | tf_op jit(solution)/shard_map/dot_general | solution.py:38
  107.4 5.6 %fusion.19 = f32[16,64,64]{2,1,0:T(8,128)S(1)} fusion(f32[64,16,1024]{2,1,0:T(8,128)S(1)} %get-tuple-element.173, s32[1024]{0:T(1024)S(1)} %bitcast.211), kind=kOutput, calls=%fused_computation.35 | convolution fusion | flops 805371904 | bytes 4460544 | tf_op jit(solution)/shard_map/dot_general | solution.py:38
  113.4 10.0 %all_to_all.29 = f32[1,16,4096]{2,0,1:T(1,128)S(1)} all-to-all(f32[1,16,4096]{2,0,1:T(1,128)S(1)} %broadcast_in_dim_reshape.5), channel_id=1, replica_groups=mesh['grp'=4,'mem'=8] {'grp'}, dimensions={1} | all-to-all | bytes 524288 | tf_op jit(solution)/shard_map/all_to_all | solution.py:66
  126.1 21.8 %psum.7 = f32[8]{0:T(128)S(1)} all-reduce(f32[8]{0:T(128)S(1)} %compare_select_fusion.3), channel_id=1, replica_groups=mesh['grp'=4,'mem'=8] {'mem'}, use_global_device_ids=true, to_apply=%region_3.4 | all-reduce | flops 8 | bytes 64 | tf_op jit(solution)/shard_map/psum | solution.py:113
  149.3 7.4 %fusion.25 = f32[16,64,64]{2,1,0:T(8,128)S(1)} fusion(f32[64,16,1024]{2,1,0:T(8,128)} %get-tuple-element.174, f32[]{:T(128)} %bitcast.34, s32[1024]{0:T(1024)S(1)} %bitcast.212), kind=kOutput, calls=%fused_computation.37 | convolution fusion | flops 805437440 | bytes 4460548 | tf_op jit(solution)/shard_map/dot_general | solution.py:38
  157.1 8.4 %all_to_all.30 = f32[1,16,4096]{2,0,1:T(1,128)S(1)} all-to-all(f32[1,16,4096]{2,0,1:T(1,128)S(1)} %mul.18371), channel_id=1, replica_groups=mesh['grp'=4,'mem'=8] {'grp'}, dimensions={1} | all-to-all | bytes 524288 | tf_op jit(solution)/shard_map/all_to_all | solution.py:65
  166.4 13.6 %all_to_all.31 = f32[8,4,4,512]{3,1,2,0:T(4,128)S(1)} all-to-all(f32[8,4,4,512]{3,1,2,0:T(4,128)S(1)} %fusion.37), channel_id=1, replica_groups=mesh['grp'=4,'mem'=8] {'mem'}, dimensions={0} | all-to-all | bytes 524288 | tf_op jit(solution)/shard_map/all_to_all | solution.py:69
  180.2 34.4 %convolution_add_fusion = f32[4,512,4096]{2,1,0:T(8,128)} fusion(f32[4,512,4096]{2,1,0:T(8,128)} %param.23, f32[32,4,512]{2,0,1:T(8,128)S(1)} %reshape.1409, f32[32,4,4096]{2,1,0:T(4,128)} %all-gather.2.cloned.1.call-done), kind=kOutput, calls=%fused_computation.23 | convolution fusion | flops 3229614080 | bytes 69468160 | tf_op jit(solution)/shard_map/mqr,mqc->qrc/dot_general | solution.py:78
  (81 shorter events, 5.0 us)
Async XLA Ops:
  6.5 79.0 %copy-start = (f32[64,1024]{1,0:T(8,128)S(1)}, f32[64,1024]{1,0:T(8,128)}, u32[]{:S(2)}) copy-start(f32[64,1024]{1,0:T(8,128)} %param.20) | copy-start | bytes 786436
  6.5 173.6 %all-gather.2.cloned.1.call-start = ((), (), s32[]{:S(2)}) async-start(), calls=%async_computation.3 | async-start | bytes 2359296 | tf_op jit(solution)/shard_map/all_gather | solution.py:81
  7.8 4.9 %copy-start.6 = (s32[1,4,64]{2,1,0:T(4,128)S(1)}, s32[1,4,64]{2,1,0:T(4,128)}, u32[]{:S(2)}) copy-start(s32[1,4,64]{2,1,0:T(4,128)} %param.16) | copy-start | bytes 3076
  7.8 4.9 %copy-start.7 = (s32[1,4,64]{2,1,0:T(4,128)S(1)}, s32[1,4,64]{2,1,0:T(4,128)}, u32[]{:S(2)}) copy-start(s32[1,4,64]{2,1,0:T(4,128)} %param.15) | copy-start | bytes 3076
  7.9 4.9 %copy-start.5 = (s32[1,4,64]{2,1,0:T(4,128)S(1)}, s32[1,4,64]{2,1,0:T(4,128)}, u32[]{:S(2)}) copy-start(s32[1,4,64]{2,1,0:T(4,128)} %param.14) | copy-start | bytes 3076
  12.8 72.7 %copy-start.4 = (s32[1,1024]{1,0:T(1,128)S(1)}, s32[1,1024]{1,0:T(1,128)}, u32[]{:S(2)}) copy-start(s32[1,1024]{1,0:T(1,128)} %param.17) | copy-start | bytes 12292
  85.5 3.8 %copy-start.3 = (f32[64,1024]{1,0:T(8,128)S(1)}, f32[64,1024]{1,0:T(8,128)}, u32[]{:S(2)}) copy-start(f32[64,1024]{1,0:T(8,128)} %param.19) | copy-start | bytes 786436
  94.1 4.7 %copy-start.2 = (f32[1024,1024]{1,0:T(8,128)S(1)}, f32[1024,1024]{1,0:T(8,128)}, u32[]{:S(2)}) copy-start(f32[1024,1024]{1,0:T(8,128)} %get-tuple-element.99) | copy-start | bytes 12582916
  180.2 34.4 %copy-start.1 = (f32[64,1024]{1,0:T(8,128)S(1)}, f32[64,1024]{1,0:T(8,128)}, u32[]{:S(2)}) copy-start(f32[64,1024]{1,0:T(8,128)} %param.20) | copy-start | bytes 786436
Sparse Core Ops, SparseCore 0:
  124.9 51.0 all-gather.1
